TPU v7x, 128 devices: a whole 4x4x4 slice. The times are simulated.
128 devices in a mesh: head: 4 (over x), seq: 32 (over z, y, core).
Axes of the slice: x: 4, y: 4, z: 4, core: 2. Of those that a mesh axis runs over, the one named last changes fastest.
Arguments:
- acts: bfloat16 [32768, 1664], P('seq'), may hold values from -40 to 40
- w_qkv: bfloat16 [3, 1664, 1664], P(None, None, 'head'), may hold values from -1 to 1
- w_out: bfloat16 [1664, 1664], P('head'), may hold values from -0.15625 to 0.15625
- gain: float32 [1664], replicated, may hold values from 0.4 to 1.6
- w_merge: bfloat16 [6656, 1664], P('head'), may hold values from -0.078125 to 0.078125
- seg_ids: int32 [8192], replicated, may hold values from 0 to 63, never falling along the last dimension, each value on 1 to 256 neighbouring positions
- pad_mask: int32 [32768], replicated, may hold values 0 or 1
- owners: int32 [8192, 1], P('seq'), may hold values from 0 to 31; in each aligned block of 256 rows (0 to 255, 256 to 511, ...) at most 16 rows name the same one
Outputs:
- routed: bfloat16 [16384, 1664], P('seq', 'head')
Inputs may be any that keep to these rules, and one draw needn't show every extreme that they name: `seg_ids`: Non-decreasing; each image covers 1 to 256 consecutive windows. `owners`: among the 256 windows of one device, at most 16 name the same owner.
All inputs are finite; a program needn't handle non-finite values.
Results may differ from a plain program's by a relative error of at most 0.0085.
Values may be sent and summed in bfloat16 or wider, within the bound.
A program may use at most 256 MiB of HBM per device.

v0:
```python
import jax
import jax.numpy as jnp
from jax import lax
from jax.sharding import PartitionSpec as P

HEAD_DIM = 104


def padded(cells, sides, width):
    for axis, dim in sides:
        count = lax.axis_size(axis)
        ends = count - 1
        head = lax.slice_in_dim(cells, 0, width, axis=dim)
        tail = lax.slice_in_dim(cells, cells.shape[dim] - width, cells.shape[dim], axis=dim)
        cells = jnp.concatenate(
            [
                lax.ppermute(tail, axis, [(i, (i + 1) % count) for i in range(ends)]),
                cells,
                lax.ppermute(head, axis, [((i + 1) % count, i) for i in range(ends)]),
            ],
            axis=dim,
        )
    return cells


def per_device(acts, w_qkv, w_out, gain, w_merge, seg_ids, pad_mask, owners):
    rows = acts.shape[0]
    width = acts.shape[1]
    local_width = w_qkv.shape[2]
    heads_here = local_width // HEAD_DIM
    seq_count = lax.axis_size("seq")
    seq_index = lax.axis_index("seq")
    head_count = lax.axis_size("head")
    head_index = lax.axis_index("head")
    projected = jnp.einsum("td,kdh->kth", acts, w_qkv, preferred_element_type=jnp.float32).astype(
        jnp.bfloat16
    )
    keyval = jnp.concatenate([projected[1], projected[2]], axis=1)
    rimmed = padded(keyval, (("seq", 0),), rows)
    seg_tokens = jnp.repeat(seg_ids, 4)
    seg_fill = jnp.full((rows,), -1, jnp.int32)
    live_fill = jnp.zeros((rows,), jnp.int32)
    seg_padded = jnp.concatenate([seg_fill, seg_tokens, seg_fill])
    live_padded = jnp.concatenate([live_fill, pad_mask, live_fill])
    first = seq_index * rows
    key_img = lax.dynamic_slice_in_dim(seg_padded, first, 3 * rows, 0)
    key_live = lax.dynamic_slice_in_dim(live_padded, first, 3 * rows, 0)
    query_img = lax.dynamic_slice_in_dim(seg_tokens, first, rows, 0)
    query_live = lax.dynamic_slice_in_dim(pad_mask, first, rows, 0)
    query_heads = projected[0].reshape(rows, heads_here, HEAD_DIM)
    scale = HEAD_DIM ** (-0.5)
    diagonal = jnp.eye(rows, dtype=bool)
    score_list = []
    allowed_list = []
    value_list = []
    touch_list = []
    for block in range(3):
        block_img = key_img[block * rows : (block + 1) * rows]
        block_live = key_live[block * rows : (block + 1) * rows]
        same_img = query_img[:, None] == block_img[None, :]
        if block == 1:
            allowed = same_img & ((block_live[None, :] == 1) | diagonal)
        else:
            allowed = same_img & (block_live[None, :] == 1)
        block_keys = rimmed[block * rows : (block + 1) * rows, :local_width].reshape(
            rows, heads_here, HEAD_DIM
        )
        block_values = rimmed[block * rows : (block + 1) * rows, local_width:].reshape(
            rows, heads_here, HEAD_DIM
        )
        touches = None
        raw = (
            jnp.einsum("qhd,khd->hqk", query_heads, block_keys, preferred_element_type=jnp.float32)
            * scale
        )
        scores = jnp.where(allowed[None], raw, -1e30)
        score_list.append(scores)
        allowed_list.append(allowed)
        value_list.append(block_values)
        touch_list.append(touches)
    highest = jnp.maximum(
        jnp.maximum(jnp.max(score_list[0], axis=2), jnp.max(score_list[1], axis=2)),
        jnp.max(score_list[2], axis=2),
    )
    total = jnp.zeros((heads_here, rows), jnp.float32)
    gathered = jnp.zeros((rows, heads_here, HEAD_DIM), jnp.float32)
    for block in range(3):
        weights = jnp.where(
            allowed_list[block][None], jnp.exp(score_list[block] - highest[:, :, None]), 0.0
        )
        total = total + jnp.sum(weights, axis=2)
        rounded = weights.astype(jnp.bfloat16)
        block_values = value_list[block]
        gathered = gathered + jnp.einsum(
            "hqk,khd->qhd", rounded, block_values, preferred_element_type=jnp.float32
        )
    attn = (gathered / jnp.transpose(total)[:, :, None]).reshape(rows, local_width)
    attn = (attn * query_live[:, None].astype(jnp.float32)).astype(jnp.bfloat16)
    windows = rows // 4
    per_head = 4 // head_count
    partial_value = jnp.dot(attn, w_out, preferred_element_type=jnp.float32).reshape(
        windows, 4, width
    )
    summed = lax.psum_scatter(partial_value, "head", scatter_dimension=1, tiled=True)
    residual = lax.dynamic_slice_in_dim(
        acts.reshape(windows, 4, width), head_index * per_head, per_head, 1
    )
    hidden = residual.astype(jnp.float32) + summed
    centre = jnp.mean(hidden, axis=2, keepdims=True)
    centered = hidden - centre
    variance = jnp.mean(centered * centered, axis=2, keepdims=True)
    normed = (centered * lax.rsqrt(variance + 1e-06) * gain[None, None, :]).astype(jnp.bfloat16)
    merge_part = jnp.dot(
        normed.reshape(windows, per_head * width), w_merge, preferred_element_type=jnp.float32
    )
    merged = lax.psum_scatter(merge_part, "head", scatter_dimension=1, tiled=True).astype(
        jnp.bfloat16
    )
    owner = owners[:, 0]
    capacity = rows // (2 * seq_count)
    hits = (owner[:, None] == jnp.arange(seq_count, dtype=jnp.int32)[None, :]).astype(jnp.int32)
    rank = jnp.sum(hits * (jnp.cumsum(hits, axis=0) - 1), axis=1)
    slot = owner * capacity + rank
    dispatch = (slot[None, :] == jnp.arange(seq_count * capacity, dtype=jnp.int32)[:, None]).astype(
        jnp.bfloat16
    )
    outgoing = jnp.dot(dispatch, merged, preferred_element_type=jnp.float32).astype(jnp.bfloat16)
    return lax.all_to_all(outgoing, "seq", split_axis=0, concat_axis=0, tiled=True)


def solution(mesh):
    in_specs = (
        P("seq", None),
        P(None, None, "head"),
        P("head", None),
        P(),
        P("head", None),
        P(),
        P(),
        P("seq", None),
    )
    out_specs = P("seq", "head")
    return jax.shard_map(
        per_device, mesh=mesh, in_specs=in_specs, out_specs=out_specs, check_vma=False
    )
```

profile of v0, /device:TPU:1, one launch (start us, length us, event | category | flops | bytes accessed | tf_op | source)
XLA Modules:
  0.0 256.0 jit_solution(2008060122078534597)
XLA Ops:
  6.5 8.2 %convert_bitcast_fusion = bf16[3,1024,416]{1,2,0:T(8,128)(2,1)S(1)} fusion(bf16[3,1664,416]{1,2,0:T(8,128)(2,1)} %param.9, bf16[1024,1664]{1,0:T(8,128)(2,1)} %param.8), kind=kOutput, calls=%fused_computation.29 | convolution fusion | flops 4254302208 | bytes 10117120 | tf_op jit(solution)/shard_map/td,kdh->kth/dot_general | solution.py:35
  14.7 1.5 fusion.53
  16.2 1.3 pad_maximum_fusion
  17.6 3.3 %collective-permute-start.1 = (bf16[1024,832]{0,1:T(8,128)(2,1)}, bf16[1024,832]{0,1:T(8,128)(2,1)}, u32[]{:S(2)}, u32[]{:S(2)}) collective-permute-start(bf16[1024,832]{0,1:T(8,128)(2,1)} %pad_maximum_fusion), channel_id=1, source_target_pairs={{1,0},{2,1},{3,2},{4,3},{5,4},{6,5},{7,6},{8,7},{9,8},{10,9},{11,1... | collective-permute-start | bytes 5111816 | tf_op jit(solution)/shard_map/ppermute | solution.py:19
  20.9 3.7 %collective-permute-start = (bf16[1024,832]{0,1:T(8,128)(2,1)}, bf16[1024,832]{0,1:T(8,128)(2,1)}, u32[]{:S(2)}, u32[]{:S(2)}) collective-permute-start(bf16[1024,832]{0,1:T(8,128)(2,1)} %pad_maximum_fusion), channel_id=1, source_target_pairs={{0,1},{1,2},{2,3},{3,4},{4,5},{5,6},{6,7},{7,8},{8,9},{9,10},{10,1... | collective-permute-start | bytes 5111816 | tf_op jit(solution)/shard_map/ppermute | solution.py:17
  24.6 5.0 %broadcast_in_dim.73 = s32[8192,4]{1,0:T(8,128)} broadcast(s32[8192]{0:T(1024)S(1)} %copy-done.4), dimensions={0} | broadcast | bytes 163840 | tf_op jit(solution)/shard_map/broadcast_in_dim | solution.py:40
  29.7 4.9 %reshape.235 = s32[32768]{0:T(1024)S(1)} reshape(s32[8192,4]{1,0:T(8,128)} %broadcast_in_dim.73) | data formatting | bytes 262144 | tf_op jit(solution)/shard_map/reshape | solution.py:40
  34.6 0.8 mul.62
  35.4 3.0 %fusion.19 = (pred[1024,1024]{0,1:T(8,128)(4,1)S(1)}, pred[1024,1024]{0,1:T(8,128)(4,1)S(1)}, pred[1024,1024]{0,1:T(8,128)(4,1)S(1)}) fusion(s32[1024]{0:T(1024)S(1)} %dynamic_slice.16, s32[1024]{0:T(1024)S(1)} %get-tuple-element.20, pred[1024]{0:T(1024)(128)(4,1)S(1)} %get-tuple-element.17, pred[1024]{0:T(1024)(128)(4,1)S(1)} %get-tuple-element.19, ...), kind=kLoop, calls=%fused_computation.23 | loop fusion | flops 8388608 | bytes 3165184 | tf_op jit(solution)/shard_map/and | solution.py:62
  38.4 8.7 %fusion.1 = (f32[4,1024]{1,0:T(4,128)S(1)}, f32[4,1024,1024]{1,2,0:T(8,128)}) fusion(pred[1024,1024]{0,1:T(8,128)(4,1)S(1)} %get-tuple-element.23, bf16[1024,4,104]{0,2,1:T(8,128)(2,1)S(1)} %bitcast.62, bf16[1024,4,104]{0,2,1:T(8,128)(2,1)} %bitcast.65), kind=kOutput, calls=%fused_computation.7 | convolution fusion | flops 884994048 | bytes 19546112 | tf_op jit(solution)/shard_map/qhd,khd->hqk/dot_general | solution.py:73
  47.2 2.4 fusion.54
  49.6 3.5 %fusion.2 = (f32[4,1024]{1,0:T(4,128)S(1)}, f32[4,1024,1024]{1,2,0:T(8,128)S(1)}) fusion(pred[1024,1024]{0,1:T(8,128)(4,1)S(1)} %get-tuple-element.24, bf16[1024,4,104]{0,2,1:T(8,128)(2,1)S(1)} %bitcast.63, bf16[1024,4,104]{0,2,1:T(8,128)(2,1)S(1)} %bitcast.67), kind=kOutput, calls=%fused_computation.8 | convolution fusion | flops 884994048 | bytes 19546112 | tf_op jit(solution)/shard_map/qhd,khd->hqk/dot_general | solution.py:73
  53.2 2.5 fusion.55
  55.7 7.8 %fusion = (f32[4,1024]{1,0:T(4,128)S(1)}, f32[4,1024,1024]{1,2,0:T(8,128)}) fusion(pred[1024,1024]{0,1:T(8,128)(4,1)S(1)} %get-tuple-element.25, bf16[1024,4,104]{0,2,1:T(8,128)(2,1)S(1)} %bitcast.64, bf16[1024,4,104]{0,2,1:T(8,128)(2,1)S(1)} %bitcast.66), kind=kOutput, calls=%fused_computation.6 | convolution fusion | flops 884994048 | bytes 19546112 | tf_op jit(solution)/shard_map/qhd,khd->hqk/dot_general | solution.py:73
  63.5 12.2 %fusion.11 = f32[4,104,1024]{2,1,0:T(8,128)} fusion(bf16[1024,4,104]{0,2,1:T(8,128)(2,1)} %bitcast.70, f32[4,1024,1024]{1,2,0:T(8,128)} %get-tuple-element.31, f32[4,1024]{1,0:T(4,128)S(1)} %maximum_maximum_fusion, pred[1024,1024]{0,1:T(8,128)(4,1)S(1)} %get-tuple-element.23), kind=kOutput, calls=%fused_computation.16 | convolution fusion | flops 893386752 | bytes 20398080 | tf_op jit(solution)/shard_map/hqk,khd->qhd/dot_general | solution.py:94
  75.7 16.3 %fusion.5 = (f32[4,1024]{1,0:T(4,128)S(1)}, f32[4,1024]{1,0:T(4,128)S(1)}, f32[4,1024]{1,0:T(4,128)S(1)}) fusion(f32[4,1024,1024]{1,2,0:T(8,128)} %get-tuple-element.31, f32[4,1024]{1,0:T(4,128)S(1)} %maximum_maximum_fusion, pred[1024,1024]{0,1:T(8,128)(4,1)S(1)} %get-tuple-element.23, f32[4,1024,1024]{1,2,0:T(8,128)} %get-tuple-element.29, ...), kind=kLoop, calls=%fused_computation.11 | loop fusion | flops 62902272 | bytes 53542912 | tf_op jit(solution)/shard_map/reduce_sum | solution.py:91
  92.0 9.9 %fusion.13 = f32[4,104,1024]{2,1,0:T(8,128)} fusion(bf16[1024,4,104]{0,2,1:T(8,128)(2,1)S(1)} %bitcast.72, f32[4,1024,1024]{1,2,0:T(8,128)} %get-tuple-element.29, f32[4,1024]{1,0:T(4,128)S(1)} %maximum_maximum_fusion, pred[1024,1024]{0,1:T(8,128)(4,1)S(1)} %get-tuple-element.25), kind=kOutput, calls=%fused_computation.17 | convolution fusion | flops 893386752 | bytes 20398080 | tf_op jit(solution)/shard_map/hqk,khd->qhd/dot_general | solution.py:94
  102.0 7.3 %bitcast_divide_fusion = f32[1024,4,104]{0,2,1:T(8,128)S(1)} fusion(f32[4,104,1024]{2,1,0:T(8,128)} %fusion.13, f32[4,104,1024]{2,1,0:T(8,128)} %fusion.11, f32[1024,4]{0,1:T(4,128)S(1)} %add_bitcast_fusion.1, bf16[1024,4,104]{0,2,1:T(8,128)(2,1)} %bitcast.71, f32[4,1024,1024]{1,2,0:T(8,128)S(1)} %get-tuple-element.27, ...), kind=kOutput, calls=%fused_computation.32 | convolution fusion | flops 894664704 | bytes 23822336 | tf_op jit(solution)/shard_map/hqk,khd->qhd/dot_general | solution.py:94
  109.3 1.9 copy.27
  111.1 2.8 %reshape.239 = f32[256,4,416]{2,1,0:T(4,128)S(1)} reshape(f32[1024,4,104]{2,1,0:T(4,128)} %copy.27) | data formatting | bytes 3407872 | tf_op jit(solution)/shard_map/reshape | solution.py:97
  114.0 1.4 multiply_convert_fusion
  115.4 4.9 %fusion.24 = f32[256,4,1664]{2,0,1:T(8,128)} fusion(bf16[416,1664]{1,0:T(8,128)(2,1)S(1)} %copy-done, bf16[256,4,416]{2,1,0:T(4,128)(2,1)S(1)} %multiply_convert_fusion), kind=kOutput, calls=%fused_computation.36 | convolution fusion | flops 1417674752 | bytes 9052160 | tf_op jit(solution)/shard_map/dot_general | solution.py:101
  120.4 7.1 %reshape.233 = bf16[256,4,1664]{2,1,0:T(4,128)(2,1)} reshape(bf16[1024,1664]{1,0:T(8,128)(2,1)} %param.8) | data formatting | bytes 6815744 | tf_op jit(solution)/shard_map/reshape | solution.py:106
  127.5 3.7 %constant_dynamic-slice_fusion = bf16[256,1,1664]{2,1,0:T(2,128)(2,1)S(1)} fusion(bf16[256,4,1664]{2,1,0:T(4,128)(2,1)} %reshape.233, s32[]{:T(128)S(6)} %select_n.30), kind=kLoop, calls=%fused_computation.74 | loop fusion | bytes 1703940 | tf_op jit(solution)/shard_map/dynamic_slice | solution.py:105
  131.2 61.1 %reduce-scatter.5.cloned.1.call-done = f32[256,1,1664]{2,0,1:T(8,128)} async-done(((f32[256,4,1664]{2,0,1:T(8,128)}), f32[256,1,1664]{2,0,1:T(8,128)}) %reduce-scatter.5.cloned.1.call-update) | async-done | bytes 1703952 | tf_op jit(solution)/shard_map/reduce_scatter | solution.py:104
  192.3 1.8 fusion.52
  194.6 6.2 %convolution_bitcast_fusion = f32[1664,256]{1,0:T(8,128)} fusion(bf16[1664,1664]{1,0:T(8,128)(2,1)} %param.12, f32[1664]{0:T(1024)S(1)} %copy-done.6, f32[256]{0:T(256)S(1)} %add_rsqrt_fusion, f32[256]{0:T(256)S(1)} %broadcast_multiply_fusion, f32[256,1,1664]{2,0,1:T(8,128)S(1)} %copy-done.1, bf16[256,1,1664]{2,1,0:T(2,128)(2,1)S(1)} %constant_dynamic-slice_fusion), kind=kOutput, calls=%fused_computation.28 | convolution fusion | flops 1420230656 | bytes 9806336
  200.9 0.6 reduce-window.6
  201.9 25.2 %reduce-scatter.7.cloned.1.call-done = f32[416,256]{1,0:T(8,128)} async-done(((f32[1664,256]{1,0:T(8,128)}), f32[416,256]{1,0:T(8,128)}) %reduce-scatter.7.cloned.1.call-update) | async-done | bytes 426000
  227.1 1.1 copy.37
  228.8 19.2 %all_to_all.12 = bf16[32,16,416]{2,1,0:T(8,128)(2,1)S(1)} all-to-all(bf16[32,16,416]{2,1,0:T(8,128)(2,1)S(1)} %bitcast.68), channel_id=1, replica_groups=mesh['head'=4,'seq'=32] {'seq'}, dimensions={0} | all-to-all | bytes 851968 | tf_op jit(solution)/shard_map/all_to_all | solution.py:128
  248.0 0.9 copy.31
  (40 shorter events, 1.6 us)
Async XLA Ops:
  6.5 108.8 %copy-start = (bf16[416,1664]{1,0:T(8,128)(2,1)S(1)}, bf16[416,1664]{1,0:T(8,128)(2,1)}, u32[]{:S(2)}) copy-start(bf16[416,1664]{1,0:T(8,128)(2,1)} %param.10) | copy-start | bytes 4153348
  6.5 185.7 %reduce-scatter.5.cloned.1.call-start = ((), (), s32[]{:S(2)}) async-start(), calls=%async_computation.3 | async-start | bytes 8519680 | tf_op jit(solution)/shard_map/reduce_scatter | solution.py:104
  14.7 9.9 %copy-start.4 = (s32[8192]{0:T(1024)S(1)}, s32[8192]{0:T(1024)}, u32[]{:S(2)}) copy-start(s32[8192]{0:T(1024)} %param.13) | copy-start | bytes 98308
  17.6 29.6 %collective-permute-start.1 = (bf16[1024,832]{0,1:T(8,128)(2,1)}, bf16[1024,832]{0,1:T(8,128)(2,1)}, u32[]{:S(2)}, u32[]{:S(2)}) collective-permute-start(bf16[1024,832]{0,1:T(8,128)(2,1)} %pad_maximum_fusion), channel_id=1, source_target_pairs={{1,0},{2,1},{3,2},{4,3},{5,4},{6,5},{7,6},{8,7},{9,8},{10,9},{11,1... | collective-permute-start | bytes 5111816 | tf_op jit(solution)/shard_map/ppermute | solution.py:19
  20.9 32.3 %collective-permute-start = (bf16[1024,832]{0,1:T(8,128)(2,1)}, bf16[1024,832]{0,1:T(8,128)(2,1)}, u32[]{:S(2)}, u32[]{:S(2)}) collective-permute-start(bf16[1024,832]{0,1:T(8,128)(2,1)} %pad_maximum_fusion), channel_id=1, source_target_pairs={{0,1},{1,2},{2,3},{3,4},{4,5},{5,6},{6,7},{7,8},{8,9},{9,10},{10,1... | collective-permute-start | bytes 5111816 | tf_op jit(solution)/shard_map/ppermute | solution.py:17
  24.6 9.9 %copy-start.3 = (s32[32768]{0:T(1024)S(1)}, s32[32768]{0:T(1024)}, u32[]{:S(2)}) copy-start(s32[32768]{0:T(1024)} %param.14) | copy-start | bytes 393220
  75.7 16.3 %copy-start.2 = (bf16[1024,416]{0,1:T(8,128)(2,1)S(1)}, bf16[1024,416]{0,1:T(8,128)(2,1)}, u32[]{:S(2)}) copy-start(bf16[1024,416]{0,1:T(8,128)(2,1)} %get-tuple-element.16) | copy-start | bytes 2555908
  120.3 106.7 %reduce-scatter.7.cloned.1.call-start = ((), (), s32[]{:S(2)}) async-start(), calls=%async_computation.4 | async-start | bytes 2129920
  131.2 63.4 %copy-start.6 = (f32[1664]{0:T(1024)S(1)}, f32[1664]{0:T(1024)}, u32[]{:S(2)}) copy-start(f32[1664]{0:T(1024)} %param.11) | copy-start | bytes 19972
  192.3 2.0 copy-start.1
  194.6 6.3 %copy-start.5 = (s32[256,1]{0,1:T(1,128)S(1)}, s32[256,1]{0,1:T(1,128)}, u32[]{:S(2)}) copy-start(s32[256,1]{0,1:T(1,128)} %param.15) | copy-start | bytes 3076
Sparse Core Ops, SparseCore 0:
  120.5 71.7 reduce-scatter.4
  201.0 26.0 reduce-scatter.6
where the time goes:
time: 260 us; the launch traced here: 256 us
  waiting for transfers between devices  86.3 us (33%)
  matrix products  69.2 us (27%)
  local copies, waits for them, and re-layouts  35.3 us (14%)
  other arithmetic  25.1 us (10%)
  blocking collectives  19.2 us (7%)
  between operations  14 us (5%)
  starting transfers between devices  7.07 us (3%)
    reduce_scatter x1, waiting for transfers between devices, per_device(): lax.psum_scatter(partial_value, 'head', scatter_dimension=1, tiled=True)  61.1 us
    dot_general x3, matrix products, per_device(): jnp.einsum('hqk,khd->qhd', rounded, block_values, preferred_element_type=...  29.5 us
    unnamed x3, waiting for transfers between devices  25.2 us
    dot_general x3, matrix products, per_device(): jnp.einsum('qhd,khd->hqk', query_heads, block_keys, preferred_element_typ...  20 us
    all_to_all x1, blocking collectives, per_device(): lax.all_to_all(outgoing, 'seq', split_axis=0, concat_axis=0, tiled=True)  19.2 us
    reduce_sum x1, other arithmetic, per_device(): total = total + jnp.sum(weights, axis=2)  16.3 us
    dot_general x1, matrix products, per_device(): jnp.einsum('td,kdh->kth', acts, w_qkv, preferred_element_type=jnp.float32)  8.15 us
    reshape x1, local copies, waits for them, and re-layouts, per_device(): acts.reshape(windows, 4, width)  7.08 us
  transfers between devices with their start and end apart: 4, of which 2 were waited for; matrix products, arithmetic and copies ran while one was open for 16% of the time, Pallas kernels for 0%

commit v1 on v0

v1 whole, which is shorter than its diff:
```python
import functools
import math

import jax
import jax.numpy as jnp
from jax import lax
from jax.experimental import pallas as pl
from jax.experimental.pallas import tpu as pltpu
from jax.sharding import PartitionSpec as P

HEAD_DIM = 104
BLK = 256
WIN = BLK // 4
NB = 4
MESH = pl.DeviceIdType.MESH
NEG = -1e30
F32 = jnp.float32
BF16 = jnp.bfloat16
K_OFF = (0, 0, 128, 256)


def iota(shape, dim):
    return lax.broadcasted_iota(jnp.int32, shape, dim)


def nt_dot(a, b):
    return lax.dot_general(a, b, (((1,), (1,)), ((), ())), preferred_element_type=F32)


def nn_dot(a, b):
    return lax.dot_general(a, b, (((1,), (0,)), ((), ())), preferred_element_type=F32)


def kernel(
    n_seq,
    n_head,
    acts_hbm,
    wqkv_hbm,
    wout_hbm,
    gain_ref,
    wmerge_hbm,
    seg_ref,
    pad_ref,
    owner_ref,
    out_hbm,
    acts,
    wst,
    wq,
    wkv,
    kv,
    qm,
    acc,
    mst,
    lst,
    bias,
    wfull,
    wmerge,
    resid,
    asend,
    arecv,
    psend,
    precv,
    outgoing,
    qimg,
    qlive,
    kcode,
    acts_sem,
    wst_sem,
    wl_sem,
    kv_ssem,
    kv_rsem,
    w1_ssem,
    w1_rsem,
    w2_ssem,
    w2_rsem,
    w3_ssem,
    w3_rsem,
    a_ssem,
    a_rsem,
    p_ssem,
    p_rsem,
    o_ssem,
    o_rsem,
    o_lsem,
):
    d = acts.shape[1]
    s = lax.axis_index("seq")
    h = lax.axis_index("head")
    core = lax.rem(s, 2)
    right = lax.rem(s + 1, n_seq)
    left = lax.rem(s + n_seq - 1, n_seq)
    partner = s + 1 - 2 * core
    hp1 = lax.rem(h + 1, n_head)
    hm1 = lax.rem(h + n_head - 1, n_head)
    hp2 = lax.rem(h + 2, n_head)

    def acts_copy(c):
        rows = pl.ds(c * BLK, BLK)
        return pltpu.make_async_copy(acts_hbm.at[rows], acts.at[rows], acts_sem.at[c])

    def wst_copy(k):
        return pltpu.make_async_copy(wqkv_hbm.at[k], wst.at[k], wst_sem.at[k])

    wst_copy(1).start()
    wst_copy(2).start()
    acts_copy(3).start()
    acts_copy(0).start()
    acts_copy(2).start()
    acts_copy(1).start()
    wst_copy(0).start()
    wout_local = pltpu.make_async_copy(wout_hbm, wfull.at[h], wl_sem.at[0])
    wout_local.start()
    wmerge_local = pltpu.make_async_copy(wmerge_hbm, wmerge, wl_sem.at[1])
    wmerge_local.start()

    barrier = pltpu.get_barrier_semaphore()
    for k in range(1, n_head):
        pl.semaphore_signal(
            barrier, inc=1, device_id={"head": lax.rem(h + k, n_head)}, device_id_type=MESH
        )

    def greet(k, carry):
        pl.semaphore_signal(
            barrier, inc=1, device_id={"seq": lax.rem(s + k, n_seq)}, device_id_type=MESH
        )
        return carry

    lax.fori_loop(1, n_seq, greet, 0)

    n_img_rows = seg_ref.shape[0]
    n_pad_rows = pad_ref.shape[0]
    expand = (iota((128, 512), 0) == iota((128, 512), 1) // 4).astype(BF16)
    expand_t = (iota((512, 128), 1) == iota((512, 128), 0) // 4).astype(BF16)
    eye = (iota((128, 128), 0) == iota((128, 128), 1)).astype(BF16)
    for r in range(6):
        row = 2 * s - 2 + r
        inside = jnp.logical_and(row >= 0, row < n_img_rows)
        safe = jnp.clip(row, 0, n_img_rows - 1)
        seg_row = seg_ref[pl.ds(safe, 1), :].astype(F32)
        seg_row = jnp.where(inside, seg_row, -1.0)
        wide = jnp.broadcast_to(seg_row, (128, 128)).astype(BF16)
        codes = nn_dot(wide[:16], expand)[:1]
        if 2 <= r < 4:
            qimg[(r - 2) * 512 : (r - 1) * 512, :] = nt_dot(expand_t, wide)
        for half in range(2):
            chunk = 2 * r + half
            for part in range(2):
                prow = 4 * (2 * s - 2 + r) + 2 * half + part
                pin = jnp.clip(prow, 0, n_pad_rows - 1)
                live = pad_ref[pl.ds(pin, 1), :].astype(F32)
                lanes = slice(half * 256 + part * 128, half * 256 + part * 128 + 128)
                code = jnp.where(jnp.logical_and(inside, live == 1.0), codes[:, lanes], -2.0)
                kcode[chunk : chunk + 1, part * 128 : part * 128 + 128] = code
                if 2 <= r < 4:
                    at = (r - 2) * 512 + half * 256 + part * 128
                    livew = jnp.broadcast_to(live, (128, 128)).astype(BF16)
                    qlive[at : at + 128, :] = nt_dot(eye, livew)

    wst_copy(1).wait()
    wst_copy(2).wait()
    wkv[:, 0:384] = wst[1, :, 0:384]
    wkv[:, 512:896] = wst[2, :, 0:384]
    wkv[:, 384:512] = jnp.concatenate(
        [wst[2, :, 384:416], wst[1, :, 384:416], jnp.zeros((d, 64), BF16)], axis=1
    )

    pl.semaphore_wait(barrier, n_seq - 1 + n_head - 1)

    half_rows = wout_hbm.shape[0] // 2
    q_rows = (half_rows // 32 + 1) * 16
    mine = pl.ds(pl.multiple_of(core * half_rows, 16), half_rows)
    first = pl.ds(pl.multiple_of(core * half_rows, 16), q_rows)
    second = pl.ds(pl.multiple_of(core * half_rows + q_rows, 16), half_rows - q_rows)

    def remote(src, dst, ssem, rsem, dev):
        return pltpu.make_async_remote_copy(
            src_ref=src, dst_ref=dst, send_sem=ssem, recv_sem=rsem, device_id=dev, device_id_type=MESH
        )

    w1 = [
        remote(
            wout_hbm.at[mine], wfull.at[h, mine], w1_ssem.at[0], w1_rsem.at[0], {"head": hp1}
        ),
        remote(
            wout_hbm.at[mine], wfull.at[h, mine], w1_ssem.at[1], w1_rsem.at[1], {"head": hm1}
        ),
    ]
    w1[0].start()
    w1[1].start()

    def halo(t):
        way = lax.rem(t, 2)
        step = t // 2
        c = jnp.where(way == 0, NB - 1 - step, step)
        dst = jnp.where(way == 0, c, 2 * NB + c)
        to = jnp.where(way == 0, right, left)
        return c, remote(
            kv.at[NB + c], kv.at[dst], kv_ssem.at[way, step], kv_rsem.at[way, step], {"seq": to}
        )

    def project_kv(t, carry):
        c, copy = halo(t)
        acts_copy(c).wait()
        rows = pl.ds(pl.multiple_of(c * BLK, BLK), BLK)
        kv[NB + c] = nn_dot(acts[rows, :], wkv[...]).astype(BF16)
        copy.start()
        return carry

    lax.fori_loop(0, NB, project_kv, 0)

    def send_rest(t, carry):
        halo(t)[1].start()
        return carry

    lax.fori_loop(NB, 2 * NB, send_rest, 0)

    wst_copy(0).wait()
    wq[:, 0:384] = wst[0, :, 0:384]
    wq[:, 384:512] = jnp.concatenate(
        [jnp.zeros((d, 32), BF16), wst[0, :, 384:416], jnp.zeros((d, 64), BF16)], axis=1
    )
    scale = math.log2(math.e) / math.sqrt(HEAD_DIM)
    pick = (iota((WIN, BLK), 1) == 4 * iota((WIN, BLK), 0) + h).astype(BF16)

    def slot_of(i):
        return jnp.where(i == 0, 2, jnp.where(i == 3, 3, i - 1))

    def project_q(i, carry):
        rows = pl.ds(pl.multiple_of(i * BLK, BLK), BLK)
        q = nn_dot(acts[rows, :], wq[...]) * scale
        lane = iota((BLK, 512), 1)
        for k in range(4):
            lo, hi = k * HEAD_DIM, (k + 1) * HEAD_DIM if k < 3 else 512
            keep = jnp.where(jnp.logical_and(lane >= lo, lane < hi), q, 0.0)
            qm[k, rows, :] = keep[:, K_OFF[k] : K_OFF[k] + 256].astype(BF16)
        out_rows = pl.ds(pl.multiple_of(slot_of(i) * WIN, WIN), WIN)
        resid[out_rows, :] = nn_dot(pick, acts[rows, :])
        return carry

    lax.fori_loop(0, NB, project_q, 0)

    def values_of(block, k):
        if k < 3:
            off = 512 + K_OFF[k]
            return block[:, off : off + 256]
        return jnp.concatenate([block[:, 768:896], block[:, 384:512]], axis=1)

    def own(i, carry):
        rows = pl.ds(pl.multiple_of(i * BLK, BLK), BLK)
        qi = qimg[rows, :]
        qi = jnp.concatenate([qi, qi], axis=1)
        ahead = iota((BLK, BLK), 1) - iota((BLK, BLK), 0)
        for c in range(NB):
            ok = jnp.logical_or(qi == kcode[NB + c : NB + c + 1, :], ahead == BLK * (i - c))
            bias[:, c * BLK : (c + 1) * BLK] = jnp.where(ok, 0.0, NEG)
        keys = kv[NB : 2 * NB].reshape(NB * BLK, 896)
        for k in range(4):
            sc = nt_dot(qm[k, rows, :], keys[:, K_OFF[k] : K_OFF[k] + 256]) + bias[...]
            m = jnp.max(sc, axis=1, keepdims=True)
            p = jnp.exp2(sc - m)
            total = jnp.sum(p, axis=1, keepdims=True)
            acc[i, k] = nn_dot(p.astype(BF16), values_of(keys, k))
            mst[i, k] = jnp.broadcast_to(m, (BLK, 128))
            lst[i, k] = jnp.broadcast_to(total, (BLK, 128))
        return carry

    lax.fori_loop(0, NB, own, 0)

    w1[0].wait()
    w1[1].wait()
    w2 = [
        remote(
            wfull.at[hm1, first], wfull.at[hm1, first], w2_ssem.at[0], w2_rsem.at[0], {"head": hp1}
        ),
        remote(
            wfull.at[hp1, second], wfull.at[hp1, second], w2_ssem.at[1], w2_rsem.at[1], {"head": hm1}
        ),
    ]
    w3 = [
        remote(wfull.at[src, mine], wfull.at[src, mine], w3_ssem.at[k], w3_rsem.at[k], {"seq": partner})
        for k, src in enumerate((hm1, hp1, hp2))
    ]
    w2[0].start()
    w2[1].start()
    w3[0].start()
    w3[1].start()

    def pair(i, j):
        rows = pl.ds(pl.multiple_of(i * BLK, BLK), BLK)
        qi = qimg[rows, :]
        qi = jnp.concatenate([qi, qi], axis=1)
        off = jnp.where(qi == kcode[pl.ds(j, 1), :], 0.0, NEG)
        keys = kv[j]
        for k in range(4):
            sc = nt_dot(qm[k, rows, :], keys[:, K_OFF[k] : K_OFF[k] + 256]) + off
            m_old = mst[i, k]
            m = jnp.maximum(m_old, jnp.max(sc, axis=1, keepdims=True))
            alpha = jnp.exp2(m_old - m)
            mm = jnp.concatenate([m, m], axis=1)
            p = jnp.exp2(sc - mm)
            lst[i, k] = lst[i, k] * alpha + jnp.sum(p, axis=1, keepdims=True)
            aa = jnp.concatenate([alpha, alpha], axis=1)
            acc[i, k] = acc[i, k] * aa + nn_dot(p.astype(BF16), values_of(keys, k))
            mst[i, k] = m

    def near(t, carry):
        halo(2 * t)[1].wait_recv()
        halo(2 * t + 1)[1].wait_recv()

        def from_left(i, c2):
            pair(i, NB - 1 - t)
            return c2

        def from_right(i, c2):
            pair(i, 2 * NB + t)
            return c2

        lax.fori_loop(0, NB - t, from_left, 0)
        lax.fori_loop(t, NB, from_right, 0)
        return carry

    order = (iota((BLK, BLK), 1) == 4 * (iota((BLK, BLK), 0) % WIN) + iota((BLK, BLK), 0) // WIN).astype(
        BF16
    )

    def attn_copies(i):
        rows = pl.ds(pl.multiple_of(slot_of(i) * WIN, WIN), WIN)
        return [
            remote(
                asend.at[lax.rem(h + k, n_head), rows],
                arecv.at[h, rows],
                a_ssem.at[i, k - 1],
                a_rsem.at[i, k - 1],
                {"head": lax.rem(h + k, n_head)},
            )
            for k in range(1, n_head)
        ]

    def finish(i):
        rows = pl.ds(pl.multiple_of(i * BLK, BLK), BLK)
        live = qlive[rows, :]
        o = []
        for k in range(4):
            inv = live / lst[i, k]
            o.append(acc[i, k] * jnp.concatenate([inv, inv], axis=1))
        lane = iota((BLK, 128), 1)
        t0 = jnp.where(lane < HEAD_DIM, o[0][:, :128], o[1][:, :128])
        t1 = jnp.where(lane + 128 < 2 * HEAD_DIM, o[1][:, 128:], o[2][:, :128])
        t2 = jnp.where(lane + 256 < 3 * HEAD_DIM, o[2][:, 128:], o[3][:, :128])
        full = jnp.concatenate([t0, t1, t2, o[3][:, 128:]], axis=1).astype(BF16)
        sorted_rows = nn_dot(order, full).astype(BF16)
        out_rows = pl.ds(pl.multiple_of(slot_of(i) * WIN, WIN), WIN)
        for p in range(4):
            asend[p, out_rows, :] = sorted_rows[p * WIN : (p + 1) * WIN, :416]
        arecv[h, out_rows, :] = asend[h, out_rows, :]
        for copy in attn_copies(i):
            copy.start()

    def finish_loop(i, carry):
        finish(i)
        return carry

    lax.fori_loop(0, NB - 1, near, 0)
    lax.fori_loop(1, 3, finish_loop, 0)
    w2[0].wait()
    w2[1].wait()
    w3[2].start()
    lax.fori_loop(NB - 1, NB, near, 0)

    def finish_ends(i, carry):
        finish(3 * i)
        return carry

    lax.fori_loop(0, 2, finish_ends, 0)

    wout_local.wait()
    wmerge_local.wait()
    for copy in w3:
        copy.wait()

    def part_copies(t):
        rows = pl.ds(pl.multiple_of(t * 128, 128), 128)
        return [
            remote(
                psend.at[lax.rem(h + k, n_head), rows],
                precv.at[h, rows],
                p_ssem.at[t, k - 1],
                p_rsem.at[t, k - 1],
                {"head": lax.rem(h + k, n_head)},
            )
            for k in range(1, n_head)
        ]

    def tail(t, carry):
        for i in (jnp.where(t == 0, 1, 0), jnp.where(t == 0, 2, 3)):
            for copy in attn_copies(i):
                copy.wait()
        rows = pl.ds(pl.multiple_of(t * 128, 128), 128)
        hidden = resid[rows, :]
        for src in range(4):
            hidden = hidden + nn_dot(arecv[src, rows, :], wfull[src])
        mean = jnp.sum(hidden, axis=1, keepdims=True) * (1.0 / d)
        centered = hidden - mean
        var = jnp.sum(centered * centered, axis=1, keepdims=True) * (1.0 / d)
        normed = (centered * lax.rsqrt(var + 1e-6) * gain_ref[...]).astype(BF16)
        prod = nn_dot(normed, wmerge[...])
        for c in range(4):
            psend[c, rows, :] = prod[:, c * 416 : (c + 1) * 416].astype(BF16)
        precv[h, rows, :] = psend[h, rows, :]
        for copy in part_copies(t):
            copy.start()
        return carry

    lax.fori_loop(0, 2, tail, 0)

    own0 = owner_ref[0:1, :].astype(F32)
    own1 = owner_ref[1:2, :].astype(F32)
    orow = jnp.concatenate([own0, own1], axis=1)
    ocol = jnp.concatenate(
        [
            nt_dot(eye, jnp.broadcast_to(own0, (128, 128)).astype(BF16)),
            nt_dot(eye, jnp.broadcast_to(own1, (128, 128)).astype(BF16)),
        ],
        axis=0,
    )
    ocol = jnp.concatenate([ocol, ocol], axis=1)
    earlier = jnp.logical_and(ocol == orow, iota((256, 256), 0) < iota((256, 256), 1))
    rank = jnp.sum(jnp.where(earlier, 1.0, 0.0), axis=0, keepdims=True)
    cap = 1024 // (2 * n_seq)
    slot = orow * float(cap) + rank
    place = (iota((n_seq * cap, 256), 0).astype(F32) == slot).astype(BF16)

    for t in range(2):
        for copy in part_copies(t):
            copy.wait()
    merged = (
        precv[0].astype(F32) + precv[1].astype(F32) + precv[2].astype(F32) + precv[3].astype(F32)
    ).astype(BF16)
    merged = jnp.concatenate([merged[128:192], merged[0:128], merged[192:256]], axis=0)
    outgoing[...] = nn_dot(place, merged).astype(BF16)

    def route(k):
        to = lax.rem(s + k, n_seq)
        return remote(
            outgoing.at[pl.ds(pl.multiple_of(to * cap, cap), cap)],
            out_hbm.at[pl.ds(pl.multiple_of(s * cap, cap), cap)],
            o_ssem.at[k],
            o_rsem.at[k],
            {"seq": to},
        )

    here = pl.ds(pl.multiple_of(s * cap, cap), cap)
    local = pltpu.make_async_copy(outgoing.at[here], out_hbm.at[here], o_lsem.at[0])
    local.start()

    def route_start(k, carry):
        route(k).start()
        return carry

    def route_wait(k, carry):
        route(k).wait()
        return carry

    def halo_done(t, carry):
        halo(t)[1].wait_send()
        return carry

    lax.fori_loop(1, n_seq, route_start, 0)
    lax.fori_loop(0, 2 * NB, halo_done, 0)
    lax.fori_loop(1, n_seq, route_wait, 0)
    local.wait()


def per_device(n_seq, n_head, acts, w_qkv, w_out, gain, w_merge, seg_ids, pad_mask, owners):
    rows, d = acts.shape
    hidden = w_qkv.shape[2]
    wins = rows // 4
    vmem = pltpu.VMEM
    dma = pltpu.SemaphoreType.DMA
    any_spec = pl.BlockSpec(memory_space=pl.ANY)
    vmem_spec = pl.BlockSpec(memory_space=pltpu.VMEM)
    return pl.pallas_call(
        functools.partial(kernel, n_seq, n_head),
        out_shape=jax.ShapeDtypeStruct((rows // 2, hidden), BF16),
        in_specs=[any_spec, any_spec, any_spec, vmem_spec, any_spec, vmem_spec, vmem_spec, vmem_spec],
        out_specs=any_spec,
        scratch_shapes=[
            vmem((rows, d), BF16),
            vmem((3, d, hidden), BF16),
            vmem((d, 512), BF16),
            vmem((d, 896), BF16),
            vmem((3 * NB, BLK, 896), BF16),
            vmem((4, rows, 256), BF16),
            vmem((NB, 4, BLK, 256), F32),
            vmem((NB, 4, BLK, 128), F32),
            vmem((NB, 4, BLK, 128), F32),
            vmem((BLK, rows), F32),
            vmem((n_head, w_out.shape[0], d), BF16),
            vmem((d, d), BF16),
            vmem((wins, d), F32),
            vmem((n_head, wins, hidden), BF16),
            vmem((n_head, wins, hidden), BF16),
            vmem((n_head, wins, hidden), BF16),
            vmem((n_head, wins, hidden), BF16),
            vmem((rows // 2, hidden), BF16),
            vmem((rows, 128), F32),
            vmem((rows, 128), F32),
            vmem((16, 256), F32),
            dma((NB,)),
            dma((3,)),
            dma((2,)),
            dma((2, NB)),
            dma((2, NB)),
            dma((2,)),
            dma((2,)),
            dma((2,)),
            dma((2,)),
            dma((3,)),
            dma((3,)),
            dma((NB, 3)),
            dma((NB, 3)),
            dma((2, 3)),
            dma((2, 3)),
            dma((n_seq,)),
            dma((n_seq,)),
            dma((1,)),
        ],
        compiler_params=pltpu.CompilerParams(
            collective_id=0, has_side_effects=True, vmem_limit_bytes=67043328
        ),
        name="block",
    )(
        acts,
        w_qkv,
        w_out,
        gain.reshape(1, d),
        w_merge,
        seg_ids.reshape(-1, 128),
        pad_mask.reshape(-1, 128),
        owners.reshape(-1, 128),
    )


def solution(mesh):
    in_specs = (
        P("seq", None),
        P(None, None, "head"),
        P("head", None),
        P(),
        P("head", None),
        P(),
        P(),
        P("seq", None),
    )
    return jax.shard_map(
        functools.partial(per_device, mesh.shape["seq"], mesh.shape["head"]),
        mesh=mesh,
        in_specs=in_specs,
        out_specs=P("seq", "head"),
        check_vma=False,
    )
```

time: 260 us -> 87.5 us (0.34); the launches traced: 256 us -> 87.2 us
  waiting for transfers between devices: 86.3 us -> 0 us
  Pallas kernels: 0 us -> 76.5 us
  matrix products: 69.2 us -> 0 us
  other arithmetic: 25.1 us -> 0 us
  local copies, waits for them, and re-layouts: 35.3 us -> 10.7 us
  blocking collectives: 19.2 us -> 0 us
  between operations: 14 us -> 0.01 us
  starting transfers between devices: 7.07 us -> 0 us
    pallas_call x0 -> x1, Pallas kernels: none -> 76.5 us  [per_device(): pl.pallas_call(functools.partial(kernel, n_seq, n_head), out_shape=jax.Sh...]
    dot_general x9 -> x0, matrix products: 63 us -> none  [the longest x3 29.5 us: per_device(): jnp.einsum('hqk,khd->qhd', rounded, block_values, preferred_element_type=...]
    reduce_scatter x1 -> x0, waiting for transfers between devices: 61.1 us -> none  [per_device(): lax.psum_scatter(partial_value, 'head', scatter_dimension=1, tiled=True)]
    unnamed x3 -> x0, waiting for transfers between devices: 25.2 us -> none
    all_to_all x1 -> x0, blocking collectives: 19.2 us -> none  [per_device(): lax.all_to_all(outgoing, 'seq', split_axis=0, concat_axis=0, tiled=True)]
    reduce_sum x4 -> x0, other arithmetic: 18.6 us -> none  [the longest x1 16.3 us: per_device(): total = total + jnp.sum(weights, axis=2)]
    reshape x3 -> x1, local copies, waits for them, and re-layouts: 14.7 us -> 1.29 us  [per_device(): gain.reshape(1, d)]
    ppermute x2 -> x0, starting transfers between devices: 7.02 us -> none  [the longest x1 3.71 us: padded(): lax.ppermute(tail, axis, [(i, (i + 1) % count) for i in range(ends)])]
  transfers between devices with their start and end apart: 4 -> 0, of which waited for: 2 -> 0; matrix products, arithmetic and copies ran while one was open for 16% -> 0% of each run, Pallas kernels for 0% -> 0%
where the time goes in v1:
time: 87.5 us; the launch traced here: 87.2 us
  Pallas kernels  76.5 us (87%)
  local copies, waits for them, and re-layouts  10.7 us (12%)
    pallas_call x1, Pallas kernels, per_device(): pl.pallas_call(functools.partial(kernel, n_seq, n_head), out_shape=jax.Sh...  76.5 us
    unnamed x1, local copies, waits for them, and re-layouts  7.39 us
    pallas_call x1, local copies, waits for them, and re-layouts, per_device(): pl.pallas_call(functools.partial(kernel, n_seq, n_head), out_shape=jax.Sh...  1.99 us

profile of v1, /device:TPU:1, one launch (start us, length us, event | category | flops | bytes accessed | tf_op | source)
XLA Modules:
  0.0 87.2 jit_solution(15108325308550183160)
XLA Ops:
  0.0 1.3 %reshape.12.gain_ref = f32[1,1664]{1,0:T(1,128)} reshape(f32[1664]{0:T(1024)} %param.11) | data formatting | bytes 13312 | tf_op jit(solution)/shard_map/reshape | solution.py:536
  1.3 7.4 %copy.9.wqkv_hbm = bf16[3,1664,416]{2,1,0:T(8,128)(2,1)} copy(bf16[3,1664,416]{1,2,0:T(8,128)(2,1)} %param.9) | data formatting | bytes 8306688 | tf_op args[1]
  8.7 76.5 %block.1 = bf16[512,416]{1,0:T(8,128)(2,1)} custom-call(bf16[1024,1664]{1,0:T(8,128)(2,1)} %acts_hbm.1, bf16[3,1664,416]{2,1,0:T(8,128)(2,1)} %copy.9.wqkv_hbm, bf16[416,1664]{1,0:T(8,128)(2,1)} %wout_hbm.1, f32[1,1664]{1,0:T(1,128)} %reshape.12.gain_ref, bf16[1664,1664]{1,0:T(8,128)(2,1)} %wmerge_hbm.1, s32[64,128]{1,0:T(8,128)} %bitcast.4, ...), custom_call_target="tpu_custom_call" | custom-call | tf_op jit(solution)/shard_map/block/pallas_call | solution.py:482
  85.2 2.0 %copy.10 = bf16[512,416]{0,1:T(8,128)(2,1)} copy(bf16[512,416]{1,0:T(8,128)(2,1)} %block.1) | data formatting | bytes 851968 | tf_op jit(solution)/shard_map/block/pallas_call | solution.py:482

commit v2 on v1

--- a/solution.py
+++ b/solution.py
@@ -44,7 +44,6 @@
     owner_ref,
     out_hbm,
     acts,
-    wst,
     wq,
     wkv,
     kv,
@@ -98,16 +97,29 @@
         rows = pl.ds(c * BLK, BLK)
         return pltpu.make_async_copy(acts_hbm.at[rows], acts.at[rows], acts_sem.at[c])
 
-    def wst_copy(k):
-        return pltpu.make_async_copy(wqkv_hbm.at[k], wst.at[k], wst_sem.at[k])
-
-    wst_copy(1).start()
-    wst_copy(2).start()
+    def w_copy(n, part, src, dst, at, size):
+        return pltpu.make_async_copy(
+            wqkv_hbm.at[part, pl.ds(src, size)], dst.at[pl.ds(at, size)], wst_sem.at[n]
+        )
+
+    kv_loads = [
+        w_copy(0, 1, 0, wkv, 0, 384),
+        w_copy(1, 2, 384, wkv, 384, 32),
+        w_copy(2, 1, 384, wkv, 416, 32),
+        w_copy(3, 2, 0, wkv, 512, 384),
+    ]
+    q_loads = [w_copy(4, 0, 0, wq, 0, 384), w_copy(5, 0, 384, wq, 416, 32)]
+    for copy in kv_loads:
+        copy.start()
     acts_copy(3).start()
     acts_copy(0).start()
     acts_copy(2).start()
     acts_copy(1).start()
-    wst_copy(0).start()
+    for copy in q_loads:
+        copy.start()
+    wkv[448:512, :] = jnp.zeros((64, d), BF16)
+    wq[384:416, :] = jnp.zeros((32, d), BF16)
+    wq[448:512, :] = jnp.zeros((64, d), BF16)
     wout_local = pltpu.make_async_copy(wout_hbm, wfull.at[h], wl_sem.at[0])
     wout_local.start()
     wmerge_local = pltpu.make_async_copy(wmerge_hbm, wmerge, wl_sem.at[1])
@@ -143,7 +155,9 @@
         if 2 <= r < 4:
             qimg[(r - 2) * 512 : (r - 1) * 512, :] = nt_dot(expand_t, wide)
         for half in range(2):
-            chunk = 2 * r + half
+            chunk = 2 * r + half if r < 2 else 2 * NB + 2 * (r - 2) + half
+            if r >= 4:
+                chunk = NB + 2 * (r - 4) + half
             for part in range(2):
                 prow = 4 * (2 * s - 2 + r) + 2 * half + part
                 pin = jnp.clip(prow, 0, n_pad_rows - 1)
@@ -156,13 +170,8 @@
                     livew = jnp.broadcast_to(live, (128, 128)).astype(BF16)
                     qlive[at : at + 128, :] = nt_dot(eye, livew)
 
-    wst_copy(1).wait()
-    wst_copy(2).wait()
-    wkv[:, 0:384] = wst[1, :, 0:384]
-    wkv[:, 512:896] = wst[2, :, 0:384]
-    wkv[:, 384:512] = jnp.concatenate(
-        [wst[2, :, 384:416], wst[1, :, 384:416], jnp.zeros((d, 64), BF16)], axis=1
-    )
+    for copy in kv_loads:
+        copy.wait()
 
     pl.semaphore_wait(barrier, n_seq - 1 + n_head - 1)
 
@@ -192,17 +201,17 @@
         way = lax.rem(t, 2)
         step = t // 2
         c = jnp.where(way == 0, NB - 1 - step, step)
-        dst = jnp.where(way == 0, c, 2 * NB + c)
+        dst = jnp.where(way == 0, c, NB + c)
         to = jnp.where(way == 0, right, left)
         return c, remote(
-            kv.at[NB + c], kv.at[dst], kv_ssem.at[way, step], kv_rsem.at[way, step], {"seq": to}
+            kv.at[2 * NB + c], kv.at[dst], kv_ssem.at[way, step], kv_rsem.at[way, step], {"seq": to}
         )
 
     def project_kv(t, carry):
         c, copy = halo(t)
         acts_copy(c).wait()
         rows = pl.ds(pl.multiple_of(c * BLK, BLK), BLK)
-        kv[NB + c] = nn_dot(acts[rows, :], wkv[...]).astype(BF16)
+        kv[2 * NB + c] = nt_dot(acts[rows, :], wkv[...]).astype(BF16)
         copy.start()
         return carry
 
@@ -214,11 +223,8 @@
 
     lax.fori_loop(NB, 2 * NB, send_rest, 0)
 
-    wst_copy(0).wait()
-    wq[:, 0:384] = wst[0, :, 0:384]
-    wq[:, 384:512] = jnp.concatenate(
-        [jnp.zeros((d, 32), BF16), wst[0, :, 384:416], jnp.zeros((d, 64), BF16)], axis=1
-    )
+    for copy in q_loads:
+        copy.wait()
     scale = math.log2(math.e) / math.sqrt(HEAD_DIM)
     pick = (iota((WIN, BLK), 1) == 4 * iota((WIN, BLK), 0) + h).astype(BF16)
 
@@ -227,7 +233,7 @@
 
     def project_q(i, carry):
         rows = pl.ds(pl.multiple_of(i * BLK, BLK), BLK)
-        q = nn_dot(acts[rows, :], wq[...]) * scale
+        q = nt_dot(acts[rows, :], wq[...]) * scale
         lane = iota((BLK, 512), 1)
         for k in range(4):
             lo, hi = k * HEAD_DIM, (k + 1) * HEAD_DIM if k < 3 else 512
@@ -251,11 +257,11 @@
         qi = jnp.concatenate([qi, qi], axis=1)
         ahead = iota((BLK, BLK), 1) - iota((BLK, BLK), 0)
         for c in range(NB):
-            ok = jnp.logical_or(qi == kcode[NB + c : NB + c + 1, :], ahead == BLK * (i - c))
+            ok = jnp.logical_or(qi == kcode[2 * NB + c : 2 * NB + c + 1, :], ahead == BLK * (i - c))
             bias[:, c * BLK : (c + 1) * BLK] = jnp.where(ok, 0.0, NEG)
-        keys = kv[NB : 2 * NB].reshape(NB * BLK, 896)
+        keys = kv[2 * NB : 3 * NB].reshape(NB * BLK, 896)
         for k in range(4):
-            sc = nt_dot(qm[k, rows, :], keys[:, K_OFF[k] : K_OFF[k] + 256]) + bias[...]
+            sc = nt_dot(qm[k, rows, :], keys[:, K_OFF[k] : K_OFF[k] + 256]) + bias[:, : NB * BLK]
             m = jnp.max(sc, axis=1, keepdims=True)
             p = jnp.exp2(sc - m)
             total = jnp.sum(p, axis=1, keepdims=True)
@@ -285,40 +291,6 @@
     w3[0].start()
     w3[1].start()
 
-    def pair(i, j):
-        rows = pl.ds(pl.multiple_of(i * BLK, BLK), BLK)
-        qi = qimg[rows, :]
-        qi = jnp.concatenate([qi, qi], axis=1)
-        off = jnp.where(qi == kcode[pl.ds(j, 1), :], 0.0, NEG)
-        keys = kv[j]
-        for k in range(4):
-            sc = nt_dot(qm[k, rows, :], keys[:, K_OFF[k] : K_OFF[k] + 256]) + off
-            m_old = mst[i, k]
-            m = jnp.maximum(m_old, jnp.max(sc, axis=1, keepdims=True))
-            alpha = jnp.exp2(m_old - m)
-            mm = jnp.concatenate([m, m], axis=1)
-            p = jnp.exp2(sc - mm)
-            lst[i, k] = lst[i, k] * alpha + jnp.sum(p, axis=1, keepdims=True)
-            aa = jnp.concatenate([alpha, alpha], axis=1)
-            acc[i, k] = acc[i, k] * aa + nn_dot(p.astype(BF16), values_of(keys, k))
-            mst[i, k] = m
-
-    def near(t, carry):
-        halo(2 * t)[1].wait_recv()
-        halo(2 * t + 1)[1].wait_recv()
-
-        def from_left(i, c2):
-            pair(i, NB - 1 - t)
-            return c2
-
-        def from_right(i, c2):
-            pair(i, 2 * NB + t)
-            return c2
-
-        lax.fori_loop(0, NB - t, from_left, 0)
-        lax.fori_loop(t, NB, from_right, 0)
-        return carry
-
     order = (iota((BLK, BLK), 1) == 4 * (iota((BLK, BLK), 0) % WIN) + iota((BLK, BLK), 0) // WIN).astype(
         BF16
     )
@@ -336,13 +308,34 @@
             for k in range(1, n_head)
         ]
 
-    def finish(i):
+    def far(n, carry):
+        i = jnp.where(n == 0, 1, jnp.where(n == 1, 2, jnp.where(n == 2, 0, 3)))
+
+        def arrived(t, c2):
+            halo(t)[1].wait_recv()
+            return c2
+
+        lax.fori_loop(jnp.where(n == 0, 0, NB + n), NB + 1 + n, arrived, 0)
         rows = pl.ds(pl.multiple_of(i * BLK, BLK), BLK)
+        qi = qimg[rows, :]
+        qi = jnp.concatenate([qi, qi], axis=1)
+        for c in range(NB + 1):
+            bias[:, c * BLK : (c + 1) * BLK] = jnp.where(qi == kcode[pl.ds(i + c, 1), :], 0.0, NEG)
+        keys = kv[pl.ds(i, NB + 1)].reshape((NB + 1) * BLK, 896)
         live = qlive[rows, :]
         o = []
         for k in range(4):
-            inv = live / lst[i, k]
-            o.append(acc[i, k] * jnp.concatenate([inv, inv], axis=1))
+            sc = nt_dot(qm[k, rows, :], keys[:, K_OFF[k] : K_OFF[k] + 256]) + bias[...]
+            m_old = mst[i, k]
+            m = jnp.maximum(m_old, jnp.max(sc, axis=1, keepdims=True))
+            alpha = jnp.exp2(m_old - m)
+            p = jnp.exp2(sc - m[:, :1])
+            inv = live / (lst[i, k] * alpha + jnp.sum(p, axis=1, keepdims=True))
+            beta = alpha * inv
+            o.append(
+                acc[i, k] * jnp.concatenate([beta, beta], axis=1)
+                + nn_dot(p.astype(BF16), values_of(keys, k)) * jnp.concatenate([inv, inv], axis=1)
+            )
         lane = iota((BLK, 128), 1)
         t0 = jnp.where(lane < HEAD_DIM, o[0][:, :128], o[1][:, :128])
         t1 = jnp.where(lane + 128 < 2 * HEAD_DIM, o[1][:, 128:], o[2][:, :128])
@@ -355,23 +348,13 @@
         arecv[h, out_rows, :] = asend[h, out_rows, :]
         for copy in attn_copies(i):
             copy.start()
-
-    def finish_loop(i, carry):
-        finish(i)
-        return carry
-
-    lax.fori_loop(0, NB - 1, near, 0)
-    lax.fori_loop(1, 3, finish_loop, 0)
+        return carry
+
+    lax.fori_loop(0, 2, far, 0)
     w2[0].wait()
     w2[1].wait()
     w3[2].start()
-    lax.fori_loop(NB - 1, NB, near, 0)
-
-    def finish_ends(i, carry):
-        finish(3 * i)
-        return carry
-
-    lax.fori_loop(0, 2, finish_ends, 0)
+    lax.fori_loop(2, 4, far, 0)
 
     wout_local.wait()
     wmerge_local.wait()
@@ -486,15 +469,14 @@
         out_specs=any_spec,
         scratch_shapes=[
             vmem((rows, d), BF16),
-            vmem((3, d, hidden), BF16),
-            vmem((d, 512), BF16),
-            vmem((d, 896), BF16),
+            vmem((512, d), BF16),
+            vmem((896, d), BF16),
             vmem((3 * NB, BLK, 896), BF16),
             vmem((4, rows, 256), BF16),
             vmem((NB, 4, BLK, 256), F32),
             vmem((NB, 4, BLK, 128), F32),
             vmem((NB, 4, BLK, 128), F32),
-            vmem((BLK, rows), F32),
+            vmem((BLK, (NB + 1) * BLK), F32),
             vmem((n_head, w_out.shape[0], d), BF16),
             vmem((d, d), BF16),
             vmem((wins, d), F32),
@@ -507,7 +489,7 @@
             vmem((rows, 128), F32),
             vmem((16, 256), F32),
             dma((NB,)),
-            dma((3,)),
+            dma((6,)),
             dma((2,)),
             dma((2, NB)),
             dma((2, NB)),
@@ -531,9 +513,9 @@
         name="block",
     )(
         acts,
-        w_qkv,
+        jnp.swapaxes(w_qkv, 1, 2),
         w_out,
-        gain.reshape(1, d),
+        gain,
         w_merge,
         seg_ids.reshape(-1, 128),
         pad_mask.reshape(-1, 128),

time: 87.5 us -> 70.5 us (0.81)
  local copies, waits for them, and re-layouts: 10.7 us -> 1.99 us
  Pallas kernels: 76.5 us -> 68.4 us
    pallas_call x1, Pallas kernels: 76.5 us -> 68.4 us  [per_device(): pl.pallas_call(functools.partial(kernel, n_seq, n_head), out_shape=jax.Sh...]
    unnamed x1 -> x0, local copies, waits for them, and re-layouts: 7.39 us -> none
    reshape x1 -> x0, local copies, waits for them, and re-layouts: 1.29 us -> none  [per_device(): gain.reshape(1, d)]
where the time goes in v2:
time: 70.5 us; the launch traced here: 70.4 us
  Pallas kernels  68.4 us (97%)
  local copies, waits for them, and re-layouts  1.99 us (3%)
    pallas_call x1, Pallas kernels, per_device(): pl.pallas_call(functools.partial(kernel, n_seq, n_head), out_shape=jax.Sh...  68.4 us
    pallas_call x1, local copies, waits for them, and re-layouts, per_device(): pl.pallas_call(functools.partial(kernel, n_seq, n_head), out_shape=jax.Sh...  1.99 us

profile of v2, /device:TPU:1, one launch (start us, length us, event | category | flops | bytes accessed | tf_op | source)
XLA Modules:
  0.0 70.4 jit_solution(10864448565785736852)
XLA Ops:
  0.0 68.4 %block.1 = bf16[512,416]{1,0:T(8,128)(2,1)} custom-call(bf16[1024,1664]{1,0:T(8,128)(2,1)} %acts_hbm.1, bf16[3,416,1664]{2,1,0:T(8,128)(2,1)} %bitcast.4, bf16[416,1664]{1,0:T(8,128)(2,1)} %wout_hbm.1, f32[1664]{0:T(1024)} %gain_ref.1, bf16[1664,1664]{1,0:T(8,128)(2,1)} %wmerge_hbm.1, s32[64,128]{1,0:T(8,128)} %bitcast.6, s32[256,128]{1,0:T(8,128)} %bitcast.5, ...), custom_call_target="tpu_custom_call" | custom-call | tf_op jit(solution)/shard_map/block/pallas_call | solution.py:465
  68.4 2.0 %copy.9 = bf16[512,416]{0,1:T(8,128)(2,1)} copy(bf16[512,416]{1,0:T(8,128)(2,1)} %block.1) | data formatting | bytes 851968 | tf_op jit(solution)/shard_map/block/pallas_call | solution.py:465

commit v3 on v2

--- a/solution.py
+++ b/solution.py
@@ -173,6 +173,16 @@
     for copy in kv_loads:
         copy.wait()
 
+    def project_kv(c):
+        acts_copy(c).wait()
+        rows = pl.ds(pl.multiple_of(c * BLK, BLK), BLK)
+        kv[2 * NB + c] = nt_dot(acts[rows, :], wkv[...]).astype(BF16)
+
+    def project_first(t, carry):
+        project_kv(jnp.where(t == 0, NB - 1, 0))
+        return carry
+
+    lax.fori_loop(0, 2, project_first, 0)
     pl.semaphore_wait(barrier, n_seq - 1 + n_head - 1)
 
     half_rows = wout_hbm.shape[0] // 2
@@ -194,9 +204,6 @@
             wout_hbm.at[mine], wfull.at[h, mine], w1_ssem.at[1], w1_rsem.at[1], {"head": hm1}
         ),
     ]
-    w1[0].start()
-    w1[1].start()
-
     def halo(t):
         way = lax.rem(t, 2)
         step = t // 2
@@ -207,15 +214,18 @@
             kv.at[2 * NB + c], kv.at[dst], kv_ssem.at[way, step], kv_rsem.at[way, step], {"seq": to}
         )
 
-    def project_kv(t, carry):
+    halo(0)[1].start()
+    halo(1)[1].start()
+    w1[0].start()
+    w1[1].start()
+
+    def project_rest(t, carry):
         c, copy = halo(t)
-        acts_copy(c).wait()
-        rows = pl.ds(pl.multiple_of(c * BLK, BLK), BLK)
-        kv[2 * NB + c] = nt_dot(acts[rows, :], wkv[...]).astype(BF16)
+        project_kv(c)
         copy.start()
         return carry
 
-    lax.fori_loop(0, NB, project_kv, 0)
+    lax.fori_loop(2, NB, project_rest, 0)
 
     def send_rest(t, carry):
         halo(t)[1].start()

time: 70.5 us -> 71 us (level)
  no operation moved by 1% of the time
where the time goes in v3:
time: 71 us; the launch traced here: 70.8 us
  Pallas kernels  68.8 us (97%)
  local copies, waits for them, and re-layouts  1.99 us (3%)
    pallas_call x1, Pallas kernels, per_device(): pl.pallas_call(functools.partial(kernel, n_seq, n_head), out_shape=jax.Sh...  68.8 us
    pallas_call x1, local copies, waits for them, and re-layouts, per_device(): pl.pallas_call(functools.partial(kernel, n_seq, n_head), out_shape=jax.Sh...  1.99 us

profile of v3, /device:TPU:1, one launch (start us, length us, event | category | flops | bytes accessed | tf_op | source)
XLA Modules:
  0.0 70.8 jit_solution(253547709410216088)
XLA Ops:
  0.0 68.8 %block.1 = bf16[512,416]{1,0:T(8,128)(2,1)} custom-call(bf16[1024,1664]{1,0:T(8,128)(2,1)} %acts_hbm.1, bf16[3,416,1664]{2,1,0:T(8,128)(2,1)} %bitcast.4, bf16[416,1664]{1,0:T(8,128)(2,1)} %wout_hbm.1, f32[1664]{0:T(1024)} %gain_ref.1, bf16[1664,1664]{1,0:T(8,128)(2,1)} %wmerge_hbm.1, s32[64,128]{1,0:T(8,128)} %bitcast.6, s32[256,128]{1,0:T(8,128)} %bitcast.5, ...), custom_call_target="tpu_custom_call" | custom-call | tf_op jit(solution)/shard_map/block/pallas_call | solution.py:475
  68.8 2.0 %copy.9 = bf16[512,416]{0,1:T(8,128)(2,1)} copy(bf16[512,416]{1,0:T(8,128)(2,1)} %block.1) | data formatting | bytes 851968 | tf_op jit(solution)/shard_map/block/pallas_call | solution.py:475

commit v4 on v2

--- a/solution.py
+++ b/solution.py
@@ -187,12 +187,8 @@
         )
 
     w1 = [
-        remote(
-            wout_hbm.at[mine], wfull.at[h, mine], w1_ssem.at[0], w1_rsem.at[0], {"head": hp1}
-        ),
-        remote(
-            wout_hbm.at[mine], wfull.at[h, mine], w1_ssem.at[1], w1_rsem.at[1], {"head": hm1}
-        ),
+        remote(wout_hbm.at[part], wfull.at[h, part], w1_ssem.at[k], w1_rsem.at[k], {"head": to})
+        for k, (part, to) in enumerate(((first, hp1), (second, hm1), (second, hp1), (first, hm1)))
     ]
     w1[0].start()
     w1[1].start()
@@ -244,6 +240,8 @@
         return carry
 
     lax.fori_loop(0, NB, project_q, 0)
+    w1[2].start()
+    w1[3].start()
 
     def values_of(block, k):
         if k < 3:
@@ -270,7 +268,7 @@
             lst[i, k] = jnp.broadcast_to(total, (BLK, 128))
         return carry
 
-    lax.fori_loop(0, NB, own, 0)
+    lax.fori_loop(0, NB // 2, own, 0)
 
     w1[0].wait()
     w1[1].wait()
@@ -288,6 +286,9 @@
     ]
     w2[0].start()
     w2[1].start()
+    lax.fori_loop(NB // 2, NB, own, 0)
+    w1[2].wait()
+    w1[3].wait()
     w3[0].start()
     w3[1].start()
 
@@ -493,8 +494,8 @@
             dma((2,)),
             dma((2, NB)),
             dma((2, NB)),
-            dma((2,)),
-            dma((2,)),
+            dma((4,)),
+            dma((4,)),
             dma((2,)),
             dma((2,)),
             dma((3,)),

time: 70.5 us -> 70.2 us (level)
  no operation moved by 1% of the time
where the time goes in v4:
time: 70.2 us; the launch traced here: 70.1 us
  Pallas kernels  68.1 us (97%)
  local copies, waits for them, and re-layouts  1.99 us (3%)
    pallas_call x1, Pallas kernels, per_device(): pl.pallas_call(functools.partial(kernel, n_seq, n_head), out_shape=jax.Sh...  68.1 us
    pallas_call x1, local copies, waits for them, and re-layouts, per_device(): pl.pallas_call(functools.partial(kernel, n_seq, n_head), out_shape=jax.Sh...  1.99 us

profile of v4, /device:TPU:1, one launch (start us, length us, event | category | flops | bytes accessed | tf_op | source)
XLA Modules:
  0.0 70.1 jit_solution(17644554954192872214)
XLA Ops:
  0.0 68.1 %block.1 = bf16[512,416]{1,0:T(8,128)(2,1)} custom-call(bf16[1024,1664]{1,0:T(8,128)(2,1)} %acts_hbm.1, bf16[3,416,1664]{2,1,0:T(8,128)(2,1)} %bitcast.4, bf16[416,1664]{1,0:T(8,128)(2,1)} %wout_hbm.1, f32[1664]{0:T(1024)} %gain_ref.1, bf16[1664,1664]{1,0:T(8,128)(2,1)} %wmerge_hbm.1, s32[64,128]{1,0:T(8,128)} %bitcast.6, s32[256,128]{1,0:T(8,128)} %bitcast.5, ...), custom_call_target="tpu_custom_call" | custom-call | tf_op jit(solution)/shard_map/block/pallas_call | solution.py:466
  68.1 2.0 %copy.9 = bf16[512,416]{0,1:T(8,128)(2,1)} copy(bf16[512,416]{1,0:T(8,128)(2,1)} %block.1) | data formatting | bytes 851968 | tf_op jit(solution)/shard_map/block/pallas_call | solution.py:466
